TPU v7x, 256 devices: a whole 4x4x8 slice. The times are simulated.
256 devices in a mesh: strip: 128 (over x, y_hi, z, core), harm: 2 (over y_lo).
Axes of the slice: x: 4, y: 4 (y_hi: 2, y_lo: 2; y = y_hi * 2 + y_lo), z: 8, core: 2. Of those that a mesh axis runs over, the one named last changes fastest.
Arguments:
- edge_map: float32 [128, 256, 256], P('strip'), may hold values from -1 to 2
- couple_map: float32 [128, 256, 256], P('strip'), may hold values from -0.1 to 0.1
- topo_rows: float32 [128, 256, 256], P('strip'), may hold values from -0.375 to 0.375
- mass: float32 [128, 256], P('strip'), may hold values from 0.001 to 0.01
- col_blocks: int32 [128, 2], P('strip'), may hold values from 0 to 7, all different within a row
- gravity: float32 [1024, 1024], P('strip', 'harm'), may hold values from -0.5 to 10, as said below
Outputs:
- sensitivity: float32 [128, 256, 1024], P('strip', None, 'harm')
- factor: float32 [1024, 1024], P('strip', 'harm')
Inputs may be any that keep to these rules, and one draw needn't show every extreme that they name: `col_blocks`: each row names 2 different blocks; every block is named by some strip. `gravity`: symmetric positive definite.
All inputs are finite; a program needn't handle non-finite values.
Results may differ from a plain program's by a relative error of at most 0.0003.
Values sent between devices are 32-bit elements; how exact they have to be, the bound alone decides.
A program may use at most 64 MiB of HBM per device.

v0:
```python
import jax
import jax.numpy as jnp
from jax import lax
from jax.sharding import PartitionSpec as P

HARMONICS = 1024
LEVELS = 2


HIGHEST = lax.Precision.HIGHEST


def from_behind(block, axis, distance):
    devices = range(lax.axis_size(axis))
    route = [((i - distance) % len(devices), i) for i in devices]
    return lax.ppermute(block, axis, route)


def spread(value, axis, source):
    kept = jnp.where(lax.axis_index(axis) == source, value, 0).astype(value.dtype)
    return lax.psum(kept, axis)


def product(left, right):
    return jnp.dot(left, right, precision=HIGHEST, preferred_element_type=jnp.float32)


def tproduct(left, right):
    return lax.dot_general(
        left, right, (((0,), (0,)), ((), ())), precision=HIGHEST, preferred_element_type=jnp.float32
    )


def solve_with(factor_low, rhs):
    return jax.scipy.linalg.cho_solve((factor_low, True), rhs)


def shards(edge_map, couple_map, topo_rows, mass, col_blocks, gravity):
    edge_block = edge_map[0]
    couple = couple_map[0]
    topo_block = topo_rows[0]
    blocks = col_blocks[0]
    coupled = topo_block.shape[1]
    harm_index = lax.axis_index("harm")
    strip_index = lax.axis_index("strip")
    col_width = HARMONICS // lax.axis_size("harm")
    low_half = harm_index == 0
    weight = tproduct(edge_block, edge_block)
    behind = from_behind(weight, "strip", 1)
    diag_block = weight + behind + tproduct(couple, couple) + jnp.diag(mass[0])
    upper_block = -weight
    lower_block = -behind
    offsets = jnp.arange(128, dtype=jnp.int32)
    target = (blocks[:, None] * 128 + offsets[None, :]).reshape(coupled)
    columns = harm_index * col_width + jnp.arange(col_width, dtype=jnp.int32)
    select_table = (target[:, None] == columns[None, :]).astype(jnp.float32)
    placed = product(topo_block, select_table)
    right_side = tproduct(couple, placed)
    for depth in range(LEVELS):
        stride = 2**depth
        factor_low = jnp.linalg.cholesky(diag_block)
        solved_lower = solve_with(factor_low, lower_block)
        solved_upper = solve_with(factor_low, upper_block)
        solved_right = solve_with(factor_low, right_side)
        from_below = from_behind((solved_lower, solved_upper, solved_right), "strip", stride)
        from_above = from_behind((solved_lower, solved_upper, solved_right), "strip", -stride)
        new_lower = -product(lower_block, from_below[0])
        new_upper = -product(upper_block, from_above[1])
        diag_block = (
            diag_block - product(lower_block, from_below[1]) - product(upper_block, from_above[0])
        )
        right_side = (
            right_side - product(lower_block, from_below[2]) - product(upper_block, from_above[2])
        )
        lower_block, upper_block = (new_lower, new_upper)
    sensitivity = solve_with(
        jnp.linalg.cholesky(diag_block + lower_block + upper_block), right_side
    )
    misfit = placed - product(couple, sensitivity)
    local_term = tproduct(topo_block, misfit)
    all_columns = jnp.arange(HARMONICS, dtype=jnp.int32)
    full_table = (target[:, None] == all_columns[None, :]).astype(jnp.float32)
    schur_term = tproduct(full_table, local_term)
    row_count = gravity.shape[0]
    row_start = strip_index * row_count
    mine_old = lax.dynamic_slice_in_dim(schur_term, row_start, row_count, 0)
    schur_term = lax.dynamic_update_slice_in_dim(schur_term, mine_old + gravity, row_start, 0)
    schur_half = lax.psum(schur_term, "strip")
    split_at = HARMONICS // 2

    def leading():
        corner = jnp.linalg.cholesky(schur_half[:split_at])
        solved = jax.scipy.linalg.solve_triangular(corner, schur_half[split_at:].T, lower=True)
        return jnp.concatenate([corner, solved.T], axis=0)

    def nothing():
        return jnp.zeros((HARMONICS, col_width), jnp.float32)

    panel_cols = lax.cond(low_half, leading, nothing)
    tail_rows = spread(panel_cols[split_at:], "harm", 0)

    def trailing():
        updated = schur_half[split_at:] - product(tail_rows, tail_rows.T)
        return jnp.concatenate([jnp.zeros((split_at, col_width), jnp.float32), updated], axis=0)

    def keep_panel():
        return panel_cols

    out_block = lax.cond(low_half, keep_panel, trailing)
    factor_rows = lax.dynamic_slice_in_dim(out_block, row_start, row_count, 0)
    return (sensitivity[None], factor_rows)


def solution(mesh):
    placed = (
        P("strip", None, None),
        P("strip", None, None),
        P("strip", None, None),
        P("strip", None),
        P("strip", None),
        P("strip", "harm"),
    )
    return jax.shard_map(
        shards,
        mesh=mesh,
        in_specs=placed,
        out_specs=(P("strip", None, "harm"), P("strip", "harm")),
        check_vma=False,
    )
```

profile of v0, /device:TPU:24, one launch (start us, length us, event | category | flops | bytes accessed | tf_op | source)
XLA Modules:
  0.0 1771.3 jit_solution(8342041345347091413)
XLA Ops:
  7.2 1.7 fusion.141
  9.9 1.5 fusion.43
  12.0 7.2 collective-permute-done
  19.9 11.7 cholesky.324
  31.7 9.8 custom-call.55
  42.0 11.7 cholesky.334
  56.0 4.6 while.16
  57.0 1.4 bitcast_dynamic-update-slice_fusion.8
  59.1 1.4 bitcast_dynamic-update-slice_fusion.8
  60.5 19.7 %custom-call.56 = f32[2,128,128]{1,2,0:T(8,128)S(1)} custom-call(f32[2,128,128]{2,1,0:T(8,128)S(1)} %get-tuple-element.74), custom_call_target="InvertDiagBlocksLowerTriangular" | custom-call | tf_op jit(solution)/shard_map/jit(_cho_solve)/triangular_solve | solution.py:35
  82.1 0.7 pad_maximum_fusion.6
  82.8 5.4 collective-permute-start.2
  89.9 0.7 pad_maximum_fusion.5
  93.8 0.8 pad_maximum_fusion.1
  94.6 4.9 collective-permute-start.10
  101.1 11.7 cholesky.351
  113.5 9.8 custom-call.58
  123.8 11.7 cholesky.361
  137.7 4.5 while.17
  138.7 1.4 bitcast_dynamic-update-slice_fusion.9
  140.8 1.4 bitcast_dynamic-update-slice_fusion.9
  142.2 19.7 %custom-call.59 = f32[2,128,128]{1,2,0:T(8,128)S(1)} custom-call(f32[2,128,128]{2,1,0:T(8,128)S(1)} %get-tuple-element.76), custom_call_target="InvertDiagBlocksLowerTriangular" | custom-call | tf_op jit(solution)/shard_map/jit(_cho_solve)/triangular_solve | solution.py:35
  161.9 1.5 convolution_negate_fusion.3
  165.3 5.6 collective-permute-start.6
  173.2 2.0 collective-permute-start.5
  175.2 2.0 fusion.127
  177.3 2.1 fusion.33
  182.0 0.8 pad_maximum_fusion.2
  182.8 3.7 collective-permute-start.12
  189.4 11.7 cholesky.378
  201.7 9.8 custom-call.61
  212.1 11.9 cholesky.388
  226.1 4.1 while.18
  226.7 1.4 bitcast_dynamic-update-slice_fusion.10
  228.8 1.4 bitcast_dynamic-update-slice_fusion.10
  230.2 19.7 %custom-call.64 = f32[2,128,128]{1,2,0:T(8,128)S(1)} custom-call(f32[2,128,128]{2,1,0:T(8,128)S(1)} %get-tuple-element.80), custom_call_target="InvertDiagBlocksLowerTriangular" | custom-call | tf_op jit(solution)/shard_map/jit(_cho_solve)/triangular_solve | solution.py:35
  249.9 2.0 fusion.143
  252.0 2.1 fusion.32
  256.7 1.0 convolution_subtract_fusion.7
  258.3 1.3 fusion.39
  259.7 1.3 copy-done.1
  261.0 1248.5 %all-reduce.6.cloned.1.call-done = f32[1024,512]{1,0:T(8,128)} async-done(((f32[1024,512]{1,0:T(8,128)}), f32[1024,512]{1,0:T(8,128)}) %all-reduce.6.cloned.1.call-update) | async-done | bytes 2097168 | tf_op jit(solution)/shard_map/psum | solution.py:88
  1509.6 2.9 conditional.2
  1512.5 1.1 slice_select_fusion
  1513.6 0.8 fusion.42
  1514.4 245.1 %all-reduce.8.cloned.1.call-done = f32[512,512]{1,0:T(8,128)} async-done(((f32[512,512]{1,0:T(8,128)}), f32[512,512]{1,0:T(8,128)}) %all-reduce.8.cloned.1.call-update) | async-done | bytes 1048592 | tf_op jit(solution)/shard_map/psum | solution.py:21
  1759.6 4.0 conditional.3
  1759.6 3.8 convolution_subtract_fusion
  (144 shorter events, 33.2 us)
Async XLA Ops:
  7.2 4.2 copy-start
  7.2 12.0 copy-start.7
  7.2 1502.4 %all-reduce.6.cloned.1.call-start = ((), (), s32[]{:S(2)}) async-start(), calls=%async_computation | async-start | bytes 4194304 | tf_op jit(solution)/shard_map/psum | solution.py:88
  9.0 10.1 collective-permute-start
  82.8 79.1 %collective-permute-start.3 = (f32[256,256]{1,0:T(8,128)}, f32[256,256]{1,0:T(8,128)}, u32[]{:S(2)}, u32[]{:S(2)}) collective-permute-start(f32[256,256]{1,0:T(8,128)} %pad_maximum_fusion.6), channel_id=1, source_target_pairs={{254,0},{0,2},{2,4},{4,6},{6,8},{8,10},{10,12},{12,14},{14,16},{16... | collective-permute-start | bytes 786440 | tf_op jit(solution)/shard_map/ppermute | solution.py:16
  82.8 16.7 collective-permute-start.2
  90.7 80.3 %collective-permute-start.4 = (f32[256,256]{1,0:T(8,128)}, f32[256,256]{1,0:T(8,128)S(1)}, u32[]{:S(2)}, u32[]{:S(2)}) collective-permute-start(f32[256,256]{1,0:T(8,128)} %pad_maximum_fusion.5), channel_id=1, source_target_pairs={{2,0},{4,2},{6,4},{8,6},{10,8},{12,10},{14,12},{16,14},{18,16},{20... | collective-permute-start | bytes 786440 | tf_op jit(solution)/shard_map/ppermute | solution.py:16
  90.7 9.6 collective-permute-start.1
  94.6 78.6 %collective-permute-start.10 = (f32[256,512]{1,0:T(8,128)}, f32[256,512]{1,0:T(8,128)}, u32[]{:S(2)}, u32[]{:S(2)}) collective-permute-start(f32[256,512]{1,0:T(8,128)} %pad_maximum_fusion.1), channel_id=1, source_target_pairs={{2,0},{4,2},{6,4},{8,6},{10,8},{12,10},{14,12},{16,14},{18,16},{20... | collective-permute-start | bytes 1572872 | tf_op jit(solution)/shard_map/ppermute | solution.py:16
  99.5 77.8 %collective-permute-start.9 = (f32[256,512]{1,0:T(8,128)}, f32[256,512]{1,0:T(8,128)}, u32[]{:S(2)}, u32[]{:S(2)}) collective-permute-start(f32[256,512]{1,0:T(8,128)} %pad_maximum_fusion.1), channel_id=1, source_target_pairs={{254,0},{0,2},{2,4},{4,6},{6,8},{8,10},{10,12},{12,14},{14,16},{16... | collective-permute-start | bytes 1572872 | tf_op jit(solution)/shard_map/ppermute | solution.py:16
  165.2 21.3 %collective-permute-start.7 = (f32[256,256]{1,0:T(8,128)S(1)}, f32[256,256]{1,0:T(8,128)S(1)}, u32[]{:S(2)}, u32[]{:S(2)}) collective-permute-start(f32[256,256]{1,0:T(8,128)S(1)} %pad_maximum_fusion.8), channel_id=1, source_target_pairs={{252,0},{254,2},{0,4},{2,6},{4,8},{6,10},{8,12},{10,14},{12,16},{1... | collective-permute-start | bytes 786440 | tf_op jit(solution)/shard_map/ppermute | solution.py:16
  165.3 22.0 %collective-permute-start.6 = (f32[256,256]{1,0:T(8,128)S(1)}, f32[256,256]{1,0:T(8,128)S(1)}, u32[]{:S(2)}, u32[]{:S(2)}) collective-permute-start(f32[256,256]{1,0:T(8,128)S(1)} %pad_maximum_fusion.8), channel_id=1, source_target_pairs={{4,0},{6,2},{8,4},{10,6},{12,8},{14,10},{16,12},{18,14},{20,16},{2... | collective-permute-start | bytes 786440 | tf_op jit(solution)/shard_map/ppermute | solution.py:16
  173.1 14.8 collective-permute-start.8
  173.2 15.3 collective-permute-start.5
  182.8 67.1 %collective-permute-start.12 = (f32[256,512]{1,0:T(8,128)}, f32[256,512]{1,0:T(8,128)}, u32[]{:S(2)}, u32[]{:S(2)}) collective-permute-start(f32[256,512]{1,0:T(8,128)} %pad_maximum_fusion.2), channel_id=1, source_target_pairs={{4,0},{6,2},{8,4},{10,6},{12,8},{14,10},{16,12},{18,14},{20,16},{2... | collective-permute-start | bytes 1572872 | tf_op jit(solution)/shard_map/ppermute | solution.py:16
  186.5 65.4 %collective-permute-start.11 = (f32[256,512]{1,0:T(8,128)}, f32[256,512]{1,0:T(8,128)}, u32[]{:S(2)}, u32[]{:S(2)}) collective-permute-start(f32[256,512]{1,0:T(8,128)} %pad_maximum_fusion.2), channel_id=1, source_target_pairs={{252,0},{254,2},{0,4},{2,6},{4,8},{6,10},{8,12},{10,14},{12,16},{1... | collective-permute-start | bytes 1572872 | tf_op jit(solution)/shard_map/ppermute | solution.py:16
  255.5 2.2 copy-start.4
  257.7 1.9 copy-start.6
  259.7 1.3 copy-start.1
  261.0 1498.6 %all-reduce.8.cloned.1.call-start = ((), (), s32[]{:S(2)}) async-start(), calls=%async_computation.1 | async-start | bytes 2097152 | tf_op jit(solution)/shard_map/psum | solution.py:21
Sparse Core Ops, SparseCore 0:
  261.1 1248.4 all-reduce.5
  1513.7 245.8 all-reduce.7
where the time goes:
time: 1780 us; the launch traced here: 1770 us
  waiting for transfers between devices  1500 us (84%)
  other arithmetic  169 us (9%)
  matrix products  40.8 us (2%)
  starting transfers between devices  22.7 us (1%)
  between operations  19.2 us (1%)
    psum x1, waiting for transfers between devices, shards(): schur_half = lax.psum(schur_term, 'strip')  1250 us
    psum x1, waiting for transfers between devices, spread(): return lax.psum(kept, axis)  245 us
    another operation x13, other arithmetic, shards(): factor_low = jnp.linalg.cholesky(diag_block)  68.7 us
    another operation x13, other arithmetic, solve_with(): return jax.scipy.linalg.cho_solve((factor_low, True), rhs)  62.3 us
  transfers between devices with their start and end apart: 15, of which 3 were waited for; matrix products, arithmetic and copies ran while one was open for 8% of the time, Pallas kernels for 0%

commit v1 on v0

v1 whole, which is shorter than its diff:
```python
import functools
import jax
import jax.numpy as jnp
from jax import lax
from jax.experimental import pallas as pl
from jax.experimental.pallas import tpu as pltpu
from jax.sharding import PartitionSpec as P

HIGHEST = lax.Precision.HIGHEST
F32 = jnp.float32
MESH = pl.DeviceIdType.MESH
N = 256
HALF = 512
NX, NYH, NZ, NC = 4, 2, 8, 2
VMEM = pltpu.VMEM


def dot(a, b):
    return lax.dot_general(a, b, (((1,), (0,)), ((), ())), precision=HIGHEST, preferred_element_type=F32)


def tdot(a, b):
    return lax.dot_general(a, b, (((0,), (0,)), ((), ())), precision=HIGHEST, preferred_element_type=F32)


def dott(a, b):
    return lax.dot_general(a, b, (((1,), (1,)), ((), ())), precision=HIGHEST, preferred_element_type=F32)


def eliminate(cols, rows, lo, nb):
    iota = lax.broadcasted_iota(jnp.int32, (nb, 128), 0)
    lane = lax.broadcasted_iota(jnp.int32, (nb, 128), 1)
    work = [rows, jnp.where(lane == lo + iota, 1.0, 0.0).astype(F32)]
    done = [[], []]
    pivots = []
    for k in range(nb):
        r = k % 8
        n = nb - 8 * (k // 8)
        pivot = jnp.broadcast_to(cols[k][r : r + 1, :], (n, 128))
        pivots.append(pivot[:8])
        mult = jnp.where(iota[:n] > r, cols[k] * (1.0 / pivot), 0.0)
        for j in range(k + 1, nb):
            at = 8 * (j // 8) - 8 * (k // 8)
            own = j - 8 * (k // 8)
            m = jnp.broadcast_to(mult[own : own + 1, :], (n - at, 128))
            cols[j] = cols[j] - cols[k][at:] * m
        for i in range(2):
            work[i] = work[i] - mult * jnp.broadcast_to(work[i][r : r + 1, :], (n, 128))
            if r == 7:
                done[i].append(work[i][:8])
                work[i] = work[i][8:]
    scales = []
    for t in range(nb // 8):
        spread = pivots[8 * t]
        for r in range(1, 8):
            spread = jnp.where(iota[:8] == r, pivots[8 * t + r], spread)
        scales.append(lax.rsqrt(spread))
    scale = jnp.concatenate(scales, 0)
    return jnp.concatenate(done[0], 0) * scale, jnp.concatenate(done[1], 0) * scale


def small_inverse(mat):
    nb, n = 32, 128
    lane = lax.broadcasted_iota(jnp.int32, (nb, n), 1)
    own = lax.broadcasted_iota(jnp.int32, (nb, n), 0)
    for p in range(n // nb):
        k0 = p * nb
        k1 = k0 + nb
        rows = mat[k0:k1, :]
        cols = [
            jnp.broadcast_to(rows[8 * (j // 8) :, k0 + j : k0 + j + 1], (nb - 8 * (j // 8), n)) for j in range(nb)
        ]
        up, unit = eliminate(cols, rows, k0, nb)
        panel = jnp.where((lane >= k0) & (lane < k1), unit, up)

        def update(a, b):
            at = lax.broadcasted_iota(jnp.int32, (b - a, n), 1)
            old = jnp.where((at >= k0) & (at < k1), 0.0, mat[a:b, :])
            mat[a:b, :] = old - tdot(up[:, a:b], panel)

        if k1 < n:
            update(k1, k1 + nb)
        if k1 + nb < n:
            update(k1 + nb, n)
        mat[k0:k1, :] = jnp.where(lane <= own + k0, panel, 0.0)


def inverse_factor(mat, pair):
    pair[0] = mat[:128, :128]

    def stage(i, carry):
        part = pair.at[i]
        small_inverse(part)

        @pl.when(i == 0)
        def _():
            low = dott(mat[128:, :128], part[...])
            mat[128:, :128] = low
            pair[1] = mat[128:, 128:] - dott(low, low)

        return carry

    lax.fori_loop(0, 2, stage, 0)
    mat[128:, :128] = -dot(pair[1], dot(mat[128:, :128], pair[0]))
    mat[:128, :128] = pair[0]
    mat[128:, 128:] = pair[1]
    mat[:128, 128:] = jnp.zeros((128, 128), F32)


def place_columns(compact, ids, first, second):
    left = jnp.where(ids == first, jnp.concatenate([compact[:, :128]] * 4, 1), 0.0)
    return left + jnp.where(ids == second, jnp.concatenate([compact[:, 128:]] * 4, 1), 0.0)


def whole_kernel(
    blocks, mass, edge_in, couple_in, topo_in, gravity, sens, out,
    edge, edge_behind, couple, topo, weight, diag, right_c, mat, low, up, pair,
    ahead, back, behind, front, right, right_ahead, right_back, right_behind, right_front,
    bc, wc, bx, wx, bz, wz, by, half0, half1, full0, full1, sym, corner, inv, update, remote,
    local_sem, nsend, nrecv, ssem, rsem,
):
    strip, harm = lax.axis_index("strip"), lax.axis_index("harm")
    c = lax.rem(strip, 2)
    z = lax.rem(strip // 2, NZ)
    yh = lax.rem(strip // 16, 2)
    x = strip // 32
    strips = NX * NYH * NZ * NC

    def at(x, yh, z, c):
        return (((x * 2 + yh) * NZ + z) * 2 + c, harm)

    def along(distance):
        return (lax.rem(strip + distance + strips, strips), harm)

    core = at(x, yh, z, 1 - c)
    xs = [at(lax.rem(x + d, NX), yh, z, c) for d in range(1, NX)]
    zs = [at(x, yh, lax.rem(z + d, NZ), c) for d in range(1, NZ)]
    ys = at(x, 1 - yh, z, c)
    mirror = (strip, 1 - harm)
    barrier = pltpu.get_barrier_semaphore()
    peers = [along(1), along(-1), along(2), along(-2), core, ys, mirror] + xs + zs
    for peer in peers:
        pl.semaphore_signal(barrier, inc=1, device_id=peer, device_id_type=MESH)
    loads = [
        pltpu.make_async_copy(src.at[0], dst, local_sem.at[i])
        for i, (src, dst) in enumerate(((edge_in, edge), (couple_in, couple), (topo_in, topo)))
    ]
    for load in loads:
        load.start()
    for load in loads:
        load.wait()

    def push(src, dst, slot, peer):
        copy = pltpu.make_async_remote_copy(
            src_ref=src, dst_ref=dst, send_sem=nsend.at[slot], recv_sem=nrecv.at[slot], device_id=peer, device_id_type=MESH
        )
        copy.start()
        return copy

    weight[...] = tdot(edge[...], edge[...])
    row = lax.broadcasted_iota(jnp.int32, (N, N), 0)
    col = lax.broadcasted_iota(jnp.int32, (N, N), 1)
    diag[...] = weight[...] + tdot(couple[...], couple[...]) + jnp.where(row == col, mass[...], 0.0)
    right_c[...] = tdot(couple[...], topo[...])
    pl.semaphore_wait(barrier, len(peers))
    move = push(edge, edge_behind, 0, along(1))
    ids = lax.broadcasted_iota(jnp.int32, (N, HALF), 1) // 128 + harm * 4
    first, second = blocks[0, 0], blocks[0, 1]
    right[...] = place_columns(right_c[...], ids, first, second)
    move.wait()

    lower = tdot(edge_behind[...], edge_behind[...])
    diag[...] = diag[...] + lower
    mat[...] = diag[...]
    edge_behind[...] = lower
    inverse_factor(mat, pair)
    low[...] = -dot(mat[...], edge_behind[...])
    up[...] = -dot(mat[...], weight[...])
    ahead[0] = tdot(up[...], low[...])
    ahead[1] = tdot(up[...], up[...])
    go_ahead = push(ahead.at[pl.ds(0, 2)], behind.at[pl.ds(0, 2)], 1, along(1))
    back[0] = tdot(low[...], up[...])
    back[1] = tdot(low[...], low[...])
    go_back = push(back.at[pl.ds(0, 2)], front.at[pl.ds(0, 2)], 2, along(-1))
    half = dot(mat[...], right_c[...])
    right_ahead[0] = place_columns(tdot(up[...], half), ids, first, second)
    right_go = push(right_ahead.at[0], right_behind.at[0], 3, along(1))
    right_back[0] = place_columns(tdot(low[...], half), ids, first, second)
    right_come = push(right_back.at[0], right_front.at[0], 4, along(-1))

    go_ahead.wait()
    go_back.wait()
    diag[...] = diag[...] - behind[1] - front[1]
    mat[...] = diag[...]
    inverse_factor(mat, pair)
    low[...] = -dot(mat[...], behind[0])
    up[...] = -dot(mat[...], front[0])
    cross = tdot(up[...], low[...])
    cross = 0.5 * (cross + cross.T)
    ahead[2] = tdot(up[...], up[...]) + cross
    go_ahead = push(ahead.at[2], behind.at[2], 5, along(2))
    back[2] = tdot(low[...], low[...]) + cross
    go_back = push(back.at[2], front.at[2], 6, along(-2))
    right_go.wait()
    right_come.wait()
    right[...] = right[...] - right_behind[0] - right_front[0]
    half = dot(mat[...], right[...])
    right_ahead[1] = tdot(up[...], half)
    right_go = push(right_ahead.at[1], right_behind.at[1], 7, along(2))
    right_back[1] = tdot(low[...], half)
    right_come = push(right_back.at[1], right_front.at[1], 8, along(-2))

    go_ahead.wait()
    go_back.wait()
    mat[...] = diag[...] - behind[2] - front[2]
    inverse_factor(mat, pair)
    right_go.wait()
    right_come.wait()
    right[...] = right[...] - right_behind[1] - right_front[1]
    sens[0] = tdot(mat[...], dot(mat[...], right[...]))
    right[...] = place_columns(topo[...], ids, first, second) - dot(couple[...], sens[0])
    right[...] = tdot(topo[...], right[...])
    for b in range(4):
        for shift, part in ((0, half0), (4, half1)):
            one = jnp.where(ids[:128] * 0 + first == b + shift, right[:128], 0.0)
            two = jnp.where(ids[:128] * 0 + second == b + shift, right[128:], 0.0)
            part[128 * b : 128 * b + 128, :] = one + two
    mine = pl.ds(pl.multiple_of(8 * lax.rem(strip, 64), 8), 8)

    @pl.when(strip < 64)
    def _():
        half0[mine, :] += gravity[...]

    @pl.when(strip >= 64)
    def _():
        half1[mine, :] += gravity[...]

    ins, outs = (half0, half1), (full0, full1)
    lanes = pl.ds(pl.multiple_of(c * 256, 256), 256)
    row_x = x * 128
    row_z = row_x + z * 16
    row_y = row_z + yh * 8

    def send(a, src, dst, slot, peer):
        copy = pltpu.make_async_remote_copy(
            src_ref=src, dst_ref=dst, send_sem=ssem.at[a, slot], recv_sem=rsem.at[a, slot], device_id=peer, device_id_type=MESH
        )
        copy.start()
        return copy

    def finish(copies):
        for copy in copies:
            copy.wait()

    def sum_core(a):
        return [send(a, ins[a].at[:, pl.ds(pl.multiple_of((1 - c) * 256, 256), 256)], bc.at[a], 0, core)]

    def sum_x(a):
        wc[a] = ins[a][:, lanes] + bc[a]
        return [
            send(a, wc.at[a, pl.ds(pl.multiple_of(lax.rem(x + d, NX) * 128, 128), 128)], bx.at[a, d - 1], d, xs[d - 1])
            for d in range(1, NX)
        ]

    def sum_z(a):
        wx[a] = wc[a, pl.ds(pl.multiple_of(row_x, 128), 128)] + bx[a, 0] + bx[a, 1] + bx[a, 2]
        return [
            send(a, wx.at[a, pl.ds(pl.multiple_of(lax.rem(z + d, NZ) * 16, 16), 16)], bz.at[a, d - 1], 3 + d, zs[d - 1])
            for d in range(1, NZ)
        ]

    def sum_y(a):
        total = wx[a, pl.ds(pl.multiple_of(z * 16, 16), 16)]
        for d in range(1, NZ):
            total = total + bz[a, d - 1]
        wz[a] = total
        return [send(a, wz.at[a, pl.ds(pl.multiple_of((1 - yh) * 8, 8), 8)], by.at[a], 11, ys)]

    def spread(a, piece, slot, targets):
        view = outs[a].at[piece, lanes]
        return [send(a, view, view, slot + i, peer) for i, peer in enumerate(targets)]

    def spread_y(a):
        piece = pl.ds(pl.multiple_of(row_y, 8), 8)
        outs[a][piece, lanes] = wz[a, pl.ds(pl.multiple_of(yh * 8, 8), 8)] + by[a]
        return spread(a, piece, 12, [ys])

    def spread_z(a):
        return spread(a, pl.ds(pl.multiple_of(row_z, 16), 16), 13, zs)

    def spread_x(a):
        return spread(a, pl.ds(pl.multiple_of(row_x, 128), 128), 20, xs)

    def spread_core(a):
        return spread(a, slice(None), 23, [core])

    steps = (sum_core, sum_x, sum_z, sum_y, spread_y, spread_z, spread_x, spread_core)
    live = [[], []]

    def advance(a, s):
        finish(live[a])
        live[a] = steps[s](a) if s < len(steps) else []

    advance(0, 0)
    advance(0, 1)
    advance(1, 0)
    advance(0, 2)
    advance(1, 1)
    advance(0, 3)
    advance(0, 4)
    advance(0, 5)
    advance(1, 2)
    advance(0, 6)
    advance(1, 3)
    advance(0, 7)
    advance(1, 4)
    advance(0, 8)
    advance(1, 5)

    sym[...] = 0.5 * (full0[...] + full0[...].T)
    corner[0] = sym[:N, :N]
    corner[1] = sym[N:, N:]
    inverse_factor(corner.at[0], pair)
    advance(1, 6)
    inv[:N, N:] = dott(sym[N:, :N], corner[0])
    corner[1] = corner[1] - dott(inv[:N, N:], inv[:N, N:])
    inverse_factor(corner.at[1], pair)
    advance(1, 7)
    inv[N:, :N] = -dot(corner[1], dot(inv[:N, N:], corner[0]))
    inv[:N, :N] = corner[0]
    inv[N:, N:] = corner[1]
    inv[:N, N:] = jnp.zeros((N, N), F32)
    advance(1, 8)
    source = jnp.where(strip < 64, sym[mine, :], full1[mine, :])
    solved = dott(source, inv[...])
    update[...] = dott(dot(solved, inv[...]), full1[...])
    cross_over = push(update, remote, 9, mirror)
    at_row = lax.broadcasted_iota(jnp.int32, (8, HALF), 0) + 8 * lax.rem(strip, 64)
    at_col = lax.broadcasted_iota(jnp.int32, (8, HALF), 1)
    solved = jnp.where((strip >= 64) | (at_col <= at_row), solved, 0.0)
    own = full1[mine, :]
    cross_over.wait()
    trailing = jnp.where(strip < 64, 0.0, own - remote[...])
    out[...] = jnp.where(harm == 0, solved, trailing)


def shards(edge_map, couple_map, topo_rows, mass, col_blocks, gravity):
    vmem = pl.BlockSpec(memory_space=pltpu.VMEM)
    hbm = pl.BlockSpec(memory_space=pl.ANY)

    def v(*dims):
        return VMEM(dims, F32)

    scratch = [v(N, N)] * 2 + [v(N, N)] * 8 + [v(2, 128, 128)]
    scratch += [v(3, N, N)] * 4 + [v(N, HALF)] + [v(2, N, HALF)] * 4
    scratch += [v(2, HALF, N), v(2, HALF, N), v(2, 3, 128, N), v(2, 128, N), v(2, 7, 16, N), v(2, 16, N), v(2, 8, N)]
    scratch += [v(HALF, HALF)] * 4 + [v(HALF, HALF), v(2, N, N), v(HALF, HALF), v(8, HALF), v(8, HALF)]
    dma = pltpu.SemaphoreType.DMA
    scratch += [dma((3,)), dma((10,)), dma((10,)), dma((2, 24)), dma((2, 24))]
    return pl.pallas_call(
        whole_kernel,
        out_shape=(jax.ShapeDtypeStruct((1, N, HALF), F32), jax.ShapeDtypeStruct((8, HALF), F32)),
        in_specs=[pl.BlockSpec(memory_space=pltpu.SMEM), vmem, hbm, hbm, hbm, vmem],
        out_specs=(vmem, vmem),
        scratch_shapes=scratch,
        compiler_params=pltpu.CompilerParams(vmem_limit_bytes=60 << 20, collective_id=0, has_side_effects=True),
    )(col_blocks, mass, edge_map, couple_map, topo_rows, gravity)


def solution(mesh):
    placed = (
        P("strip", None, None),
        P("strip", None, None),
        P("strip", None, None),
        P("strip", None),
        P("strip", None),
        P("strip", "harm"),
    )
    return jax.shard_map(
        shards,
        mesh=mesh,
        in_specs=placed,
        out_specs=(P("strip", None, "harm"), P("strip", "harm")),
        check_vma=False,
    )
```

time: 1780 us -> 133 us (0.07)
  waiting for transfers between devices: 1500 us -> 0 us
  other arithmetic: 169 us -> 0 us
  Pallas kernels: 0 us -> 129 us
  matrix products: 40.8 us -> 0 us
  starting transfers between devices: 22.7 us -> 0 us
  between operations: 19.2 us -> 0.65 us
    psum x2 -> x0, waiting for transfers between devices: 1490 us -> none  [the longest x1 1250 us: shards(): schur_half = lax.psum(schur_term, 'strip')]
    another operation x33 -> x0, other arithmetic: 166 us -> none  [the longest x13 68.7 us: shards(): factor_low = jnp.linalg.cholesky(diag_block)]
    pallas_call x0 -> x1, Pallas kernels: none -> 129 us  [shards(): pl.pallas_call(whole_kernel, out_shape=(jax.ShapeDtypeStruct((1, N, HALF)...]
    dot_general x20 -> x0, matrix products: 24.6 us -> none  [the longest x15 19.9 us: product(): jnp.dot(left, right, precision=HIGHEST, preferred_element_type=jnp.float32)]
    ppermute x13 -> x0, starting transfers between devices: 22.6 us -> none  [from_behind(): return lax.ppermute(block, axis, route)]
  transfers between devices with their start and end apart: 15 -> 0, of which waited for: 3 -> 0; matrix products, arithmetic and copies ran while one was open for 8% -> 0% of each run, Pallas kernels for 0% -> 0%
where the time goes in v1:
time: 133 us; the launch traced here: 132 us
  Pallas kernels  129 us (97%)
  local copies, waits for them, and re-layouts  2.48 us (2%)
    pallas_call x1, Pallas kernels, shards(): pl.pallas_call(whole_kernel, out_shape=(jax.ShapeDtypeStruct((1, N, HALF)...  129 us

profile of v1, /device:TPU:24, one launch (start us, length us, event | category | flops | bytes accessed | tf_op | source)
XLA Modules:
  0.0 131.8 jit_solution(10725760321660366452)
XLA Ops:
  0.6 128.7 %shard_map.77 = (f32[1,256,512]{2,1,0:T(8,128)}, f32[8,512]{1,0:T(8,128)}) custom-call(s32[1,2]{1,0:T(1,128)} %blocks.1, f32[1,256]{1,0:T(1,128)} %mass.1, f32[1,256,256]{2,1,0:T(8,128)} %edge_in.1, f32[1,256,256]{2,1,0:T(8,128)} %couple_in.1, f32[1,256,256]{2,1,0:T(8,128)} %topo_in.1, f32[8,512]{1,0:T(8,128)} %gravity.1), custom_call_target="tpu_custom_call" | custom-call | tf_op jit(solution)/shard_map/pallas_call | solution.py:360
  129.3 0.0 copy-start
  129.3 1.9 %copy.10 = f32[1,256,512]{2,1,0:T(8,128)} copy(f32[1,256,512]{2,1,0:T(8,128)} %get-tuple-element.4) | data formatting | bytes 1048576
  131.2 0.0 copy-done
  131.2 0.6 copy.11
Async XLA Ops:
  129.3 1.9 %copy-start = (f32[8,512]{1,0:T(8,128)S(1)}, f32[8,512]{1,0:T(8,128)}, u32[]{:S(2)}) copy-start(f32[8,512]{1,0:T(8,128)} %get-tuple-element.5) | copy-start | bytes 49156

commit v2 on v1

--- a/solution.py
+++ b/solution.py
@@ -85,22 +85,26 @@
         mat[k0:k1, :] = jnp.where(lane <= own + k0, panel, 0.0)
 
 
-def inverse_factor(mat, pair):
+def inverse_factor(mat, pair, between=None):
     pair[0] = mat[:128, :128]
 
+    def middle():
+        low = dott(mat[128:, :128], pair[0])
+        mat[128:, :128] = low
+        pair[1] = mat[128:, 128:] - dott(low, low)
+
     def stage(i, carry):
-        part = pair.at[i]
-        small_inverse(part)
-
-        @pl.when(i == 0)
-        def _():
-            low = dott(mat[128:, :128], part[...])
-            mat[128:, :128] = low
-            pair[1] = mat[128:, 128:] - dott(low, low)
-
+        small_inverse(pair.at[i])
+        pl.when(i == 0)(middle)
         return carry
 
-    lax.fori_loop(0, 2, stage, 0)
+    if between is None:
+        lax.fori_loop(0, 2, stage, 0)
+    else:
+        small_inverse(pair.at[0])
+        middle()
+        between()
+        small_inverse(pair.at[1])
     mat[128:, :128] = -dot(pair[1], dot(mat[128:, :128], pair[0]))
     mat[:128, :128] = pair[0]
     mat[128:, 128:] = pair[1]
@@ -116,8 +120,7 @@
     blocks, mass, edge_in, couple_in, topo_in, gravity, sens, out,
     edge, edge_behind, couple, topo, weight, diag, right_c, mat, low, up, pair,
     ahead, back, behind, front, right, right_ahead, right_back, right_behind, right_front,
-    bc, wc, bx, wx, bz, wz, by, half0, half1, full0, full1, sym, corner, inv, update, remote,
-    local_sem, nsend, nrecv, ssem, rsem,
+    half0, half1, cross01, sym, corner, inv, update, remote, local_sem, nsend, nrecv, *rest,
 ):
     strip, harm = lax.axis_index("strip"), lax.axis_index("harm")
     c = lax.rem(strip, 2)
@@ -157,6 +160,15 @@
         copy.start()
         return copy
 
+    lower_parts = ((slice(0, 128), slice(0, 128)), (slice(128, 256), slice(0, 256)))
+
+    def push_lower(src, dst, slot, peer):
+        return [push(src.at[rows, cols], dst.at[rows, cols], slot + i, peer) for i, (rows, cols) in enumerate(lower_parts)]
+
+    def finish(copies):
+        for copy in copies:
+            copy.wait()
+
     weight[...] = tdot(edge[...], edge[...])
     row = lax.broadcasted_iota(jnp.int32, (N, N), 0)
     col = lax.broadcasted_iota(jnp.int32, (N, N), 1)
@@ -176,43 +188,47 @@
     inverse_factor(mat, pair)
     low[...] = -dot(mat[...], edge_behind[...])
     up[...] = -dot(mat[...], weight[...])
-    ahead[0] = tdot(up[...], low[...])
-    ahead[1] = tdot(up[...], up[...])
-    go_ahead = push(ahead.at[pl.ds(0, 2)], behind.at[pl.ds(0, 2)], 1, along(1))
-    back[0] = tdot(low[...], up[...])
-    back[1] = tdot(low[...], low[...])
-    go_back = push(back.at[pl.ds(0, 2)], front.at[pl.ds(0, 2)], 2, along(-1))
+    ahead[0] = tdot(up[...], up[...])
+    go_ahead = push_lower(ahead.at[0], behind.at[0], 1, along(1))
+    back[0] = tdot(low[...], low[...])
+    go_back = push_lower(back.at[0], front.at[0], 3, along(-1))
+    ahead[1] = tdot(up[...], low[...])
+    cross_ahead = push(ahead.at[1], behind.at[1], 5, along(1))
+    back[1] = tdot(low[...], up[...])
+    cross_back = push(back.at[1], front.at[1], 6, along(-1))
     half = dot(mat[...], right_c[...])
     right_ahead[0] = place_columns(tdot(up[...], half), ids, first, second)
-    right_go = push(right_ahead.at[0], right_behind.at[0], 3, along(1))
+    right_go = push(right_ahead.at[0], right_behind.at[0], 7, along(1))
     right_back[0] = place_columns(tdot(low[...], half), ids, first, second)
-    right_come = push(right_back.at[0], right_front.at[0], 4, along(-1))
-
-    go_ahead.wait()
-    go_back.wait()
-    diag[...] = diag[...] - behind[1] - front[1]
-    mat[...] = diag[...]
+    right_come = push(right_back.at[0], right_front.at[0], 8, along(-1))
+
+    finish(go_ahead + go_back)
+    for rows, cols in lower_parts:
+        diag[rows, cols] = diag[rows, cols] - behind[0, rows, cols] - front[0, rows, cols]
+        mat[rows, cols] = diag[rows, cols]
     inverse_factor(mat, pair)
-    low[...] = -dot(mat[...], behind[0])
-    up[...] = -dot(mat[...], front[0])
+    cross_ahead.wait()
+    cross_back.wait()
+    low[...] = -dot(mat[...], behind[1])
+    up[...] = -dot(mat[...], front[1])
     cross = tdot(up[...], low[...])
     cross = 0.5 * (cross + cross.T)
     ahead[2] = tdot(up[...], up[...]) + cross
-    go_ahead = push(ahead.at[2], behind.at[2], 5, along(2))
+    go_ahead = push_lower(ahead.at[2], behind.at[2], 9, along(2))
     back[2] = tdot(low[...], low[...]) + cross
-    go_back = push(back.at[2], front.at[2], 6, along(-2))
+    go_back = push_lower(back.at[2], front.at[2], 11, along(-2))
     right_go.wait()
     right_come.wait()
     right[...] = right[...] - right_behind[0] - right_front[0]
     half = dot(mat[...], right[...])
     right_ahead[1] = tdot(up[...], half)
-    right_go = push(right_ahead.at[1], right_behind.at[1], 7, along(2))
+    right_go = push(right_ahead.at[1], right_behind.at[1], 13, along(2))
     right_back[1] = tdot(low[...], half)
-    right_come = push(right_back.at[1], right_front.at[1], 8, along(-2))
-
-    go_ahead.wait()
-    go_back.wait()
-    mat[...] = diag[...] - behind[2] - front[2]
+    right_come = push(right_back.at[1], right_front.at[1], 14, along(-2))
+
+    finish(go_ahead + go_back)
+    for rows, cols in lower_parts:
+        mat[rows, cols] = diag[rows, cols] - behind[2, rows, cols] - front[2, rows, cols]
     inverse_factor(mat, pair)
     right_go.wait()
     right_come.wait()
@@ -235,112 +251,108 @@
     def _():
         half1[mine, :] += gravity[...]
 
-    ins, outs = (half0, half1), (full0, full1)
-    lanes = pl.ds(pl.multiple_of(c * 256, 256), 256)
-    row_x = x * 128
-    row_z = row_x + z * 16
-    row_y = row_z + yh * 8
-
-    def send(a, src, dst, slot, peer):
+    cross01[...] = 0.5 * (half0[N:, :N] + half0[:N, N:].T)
+    chunks = [half0.at[:N, :N], cross01, half0.at[N:, N:], half1.at[:, :N], half1.at[:, N:]]
+    sizes = (N, N, N, HALF, HALF)
+    spaces = [rest[8 * q : 8 * q + 8] for q in range(5)]
+    ssem, rsem = rest[40], rest[41]
+    mine_lanes = pl.ds(pl.multiple_of(c * 128, 128), 128)
+    other_lanes = pl.ds(pl.multiple_of((1 - c) * 128, 128), 128)
+
+    def send(q, src, dst, slot, peer):
         copy = pltpu.make_async_remote_copy(
-            src_ref=src, dst_ref=dst, send_sem=ssem.at[a, slot], recv_sem=rsem.at[a, slot], device_id=peer, device_id_type=MESH
+            src_ref=src, dst_ref=dst, send_sem=ssem.at[q, slot], recv_sem=rsem.at[q, slot], device_id=peer, device_id_type=MESH
         )
         copy.start()
         return copy
 
-    def finish(copies):
-        for copy in copies:
-            copy.wait()
-
-    def sum_core(a):
-        return [send(a, ins[a].at[:, pl.ds(pl.multiple_of((1 - c) * 256, 256), 256)], bc.at[a], 0, core)]
-
-    def sum_x(a):
-        wc[a] = ins[a][:, lanes] + bc[a]
+    def block(index, size):
+        return pl.ds(pl.multiple_of(index * size, size), size)
+
+    def sum_core(q):
+        bc = spaces[q][0]
+        return [send(q, chunks[q].at[:, other_lanes], bc, 0, core)]
+
+    def sum_x(q):
+        bc, wc, bx = spaces[q][:3]
+        size = sizes[q] // NX
+        wc[...] = chunks[q][:, mine_lanes] + bc[...]
         return [
-            send(a, wc.at[a, pl.ds(pl.multiple_of(lax.rem(x + d, NX) * 128, 128), 128)], bx.at[a, d - 1], d, xs[d - 1])
-            for d in range(1, NX)
+            send(q, wc.at[block(lax.rem(x + d, NX), size)], bx.at[d - 1], d, xs[d - 1]) for d in range(1, NX)
         ]
 
-    def sum_z(a):
-        wx[a] = wc[a, pl.ds(pl.multiple_of(row_x, 128), 128)] + bx[a, 0] + bx[a, 1] + bx[a, 2]
+    def sum_z(q):
+        wc, bx, wx, bz = spaces[q][1:5]
+        size = sizes[q] // NX // NZ
+        wx[...] = wc[block(x, sizes[q] // NX), :] + bx[0] + bx[1] + bx[2]
         return [
-            send(a, wx.at[a, pl.ds(pl.multiple_of(lax.rem(z + d, NZ) * 16, 16), 16)], bz.at[a, d - 1], 3 + d, zs[d - 1])
-            for d in range(1, NZ)
+            send(q, wx.at[block(lax.rem(z + d, NZ), size)], bz.at[d - 1], 3 + d, zs[d - 1]) for d in range(1, NZ)
         ]
 
-    def sum_y(a):
-        total = wx[a, pl.ds(pl.multiple_of(z * 16, 16), 16)]
+    def sum_y(q):
+        wx, bz, wz, by = spaces[q][3:7]
+        total = wx[block(z, sizes[q] // NX // NZ), :]
         for d in range(1, NZ):
-            total = total + bz[a, d - 1]
-        wz[a] = total
-        return [send(a, wz.at[a, pl.ds(pl.multiple_of((1 - yh) * 8, 8), 8)], by.at[a], 11, ys)]
-
-    def spread(a, piece, slot, targets):
-        view = outs[a].at[piece, lanes]
-        return [send(a, view, view, slot + i, peer) for i, peer in enumerate(targets)]
-
-    def spread_y(a):
-        piece = pl.ds(pl.multiple_of(row_y, 8), 8)
-        outs[a][piece, lanes] = wz[a, pl.ds(pl.multiple_of(yh * 8, 8), 8)] + by[a]
-        return spread(a, piece, 12, [ys])
-
-    def spread_z(a):
-        return spread(a, pl.ds(pl.multiple_of(row_z, 16), 16), 13, zs)
-
-    def spread_x(a):
-        return spread(a, pl.ds(pl.multiple_of(row_x, 128), 128), 20, xs)
-
-    def spread_core(a):
-        return spread(a, slice(None), 23, [core])
-
-    steps = (sum_core, sum_x, sum_z, sum_y, spread_y, spread_z, spread_x, spread_core)
-    live = [[], []]
-
-    def advance(a, s):
-        finish(live[a])
-        live[a] = steps[s](a) if s < len(steps) else []
-
-    advance(0, 0)
-    advance(0, 1)
-    advance(1, 0)
-    advance(0, 2)
-    advance(1, 1)
-    advance(0, 3)
-    advance(0, 4)
-    advance(0, 5)
-    advance(1, 2)
-    advance(0, 6)
-    advance(1, 3)
-    advance(0, 7)
-    advance(1, 4)
-    advance(0, 8)
-    advance(1, 5)
-
-    sym[...] = 0.5 * (full0[...] + full0[...].T)
+            total = total + bz[d - 1]
+        wz[...] = total
+        return [send(q, wz, by, 11, ys)]
+
+    def spread(q, piece, lanes, slot, targets):
+        view = spaces[q][7].at[piece, lanes]
+        return [send(q, view, view, slot + i, peer) for i, peer in enumerate(targets)]
+
+    def spread_z(q):
+        wz, by, full = spaces[q][5:8]
+        piece = block(x * NZ + z, sizes[q] // NX // NZ)
+        full[piece, mine_lanes] = wz[...] + by[...]
+        return spread(q, piece, mine_lanes, 12, zs)
+
+    def spread_x(q):
+        return spread(q, block(x, sizes[q] // NX), mine_lanes, 19, xs)
+
+    def spread_core(q):
+        return spread(q, slice(None), mine_lanes, 22, [core])
+
+    steps = (sum_core, sum_x, sum_z, sum_y, spread_z, spread_x, spread_core)
+    live = [[], [], [], [], []]
+
+    def tick(t):
+        for q in range(5):
+            s = t - q
+            if 0 <= s <= len(steps):
+                finish(live[q])
+                live[q] = steps[s](q) if s < len(steps) else []
+
+    for t in range(8):
+        tick(t)
+
+    full = [space[7] for space in spaces]
+    sym[:N, :N] = 0.5 * (full[0][...] + full[0][...].T)
+    sym[:N, N:] = jnp.zeros((N, N), F32)
     corner[0] = sym[:N, :N]
-    corner[1] = sym[N:, N:]
-    inverse_factor(corner.at[0], pair)
-    advance(1, 6)
+    inverse_factor(corner.at[0], pair, lambda: tick(8))
+    tick(9)
+    sym[N:, :N] = full[1][...]
+    sym[N:, N:] = 0.5 * (full[2][...] + full[2][...].T)
     inv[:N, N:] = dott(sym[N:, :N], corner[0])
-    corner[1] = corner[1] - dott(inv[:N, N:], inv[:N, N:])
-    inverse_factor(corner.at[1], pair)
-    advance(1, 7)
+    corner[1] = sym[N:, N:] - dott(inv[:N, N:], inv[:N, N:])
+    inverse_factor(corner.at[1], pair, lambda: tick(10))
+    tick(11)
     inv[N:, :N] = -dot(corner[1], dot(inv[:N, N:], corner[0]))
     inv[:N, :N] = corner[0]
     inv[N:, N:] = corner[1]
     inv[:N, N:] = jnp.zeros((N, N), F32)
-    advance(1, 8)
-    source = jnp.where(strip < 64, sym[mine, :], full1[mine, :])
+    bottom_rows = jnp.concatenate([full[3][mine, :], full[4][mine, :]], 1)
+    source = jnp.where(strip < 64, sym[mine, :], bottom_rows)
     solved = dott(source, inv[...])
-    update[...] = dott(dot(solved, inv[...]), full1[...])
-    cross_over = push(update, remote, 9, mirror)
+    back_solved = dot(solved, inv[...])
+    update[...] = dott(back_solved[:, :N], full[3][...]) + dott(back_solved[:, N:], full[4][...])
+    cross_over = push(update, remote, 15, mirror)
     at_row = lax.broadcasted_iota(jnp.int32, (8, HALF), 0) + 8 * lax.rem(strip, 64)
     at_col = lax.broadcasted_iota(jnp.int32, (8, HALF), 1)
     solved = jnp.where((strip >= 64) | (at_col <= at_row), solved, 0.0)
-    own = full1[mine, :]
     cross_over.wait()
-    trailing = jnp.where(strip < 64, 0.0, own - remote[...])
+    trailing = jnp.where(strip < 64, 0.0, bottom_rows - remote[...])
     out[...] = jnp.where(harm == 0, solved, trailing)
 
 
@@ -353,10 +365,13 @@
 
     scratch = [v(N, N)] * 2 + [v(N, N)] * 8 + [v(2, 128, 128)]
     scratch += [v(3, N, N)] * 4 + [v(N, HALF)] + [v(2, N, HALF)] * 4
-    scratch += [v(2, HALF, N), v(2, HALF, N), v(2, 3, 128, N), v(2, 128, N), v(2, 7, 16, N), v(2, 16, N), v(2, 8, N)]
-    scratch += [v(HALF, HALF)] * 4 + [v(HALF, HALF), v(2, N, N), v(HALF, HALF), v(8, HALF), v(8, HALF)]
     dma = pltpu.SemaphoreType.DMA
-    scratch += [dma((3,)), dma((10,)), dma((10,)), dma((2, 24)), dma((2, 24))]
+    scratch += [v(HALF, HALF), v(HALF, HALF), v(N, N), v(HALF, HALF), v(2, N, N), v(HALF, HALF), v(8, HALF), v(8, HALF)]
+    scratch += [dma((3,)), dma((16,)), dma((16,))]
+    for n in (N, N, N, HALF, HALF):
+        m, k = n // NX, n // NX // NZ
+        scratch += [v(n, 128), v(n, 128), v(3, m, 128), v(m, 128), v(7, k, 128), v(k, 128), v(k, 128), v(n, N)]
+    scratch += [dma((5, 23)), dma((5, 23))]
     return pl.pallas_call(
         whole_kernel,
         out_shape=(jax.ShapeDtypeStruct((1, N, HALF), F32), jax.ShapeDtypeStruct((8, HALF), F32)),

time: 133 us -> 124 us (0.932)
  Pallas kernels: 129 us -> 119 us
    pallas_call x1, Pallas kernels: 129 us -> 119 us  [shards(): pl.pallas_call(whole_kernel, out_shape=(jax.ShapeDtypeStruct((1, N, HALF)...]
where the time goes in v2:
time: 124 us; the launch traced here: 122 us
  Pallas kernels  119 us (96%)
  local copies, waits for them, and re-layouts  2.48 us (2%)
    pallas_call x1, Pallas kernels, shards(): pl.pallas_call(whole_kernel, out_shape=(jax.ShapeDtypeStruct((1, N, HALF)...  119 us
    unnamed x4, local copies, waits for them, and re-layouts  2.48 us

profile of v2, /device:TPU:24, one launch (start us, length us, event | category | flops | bytes accessed | tf_op | source)
XLA Modules:
  0.0 122.0 jit_solution(8116210042328539086)
XLA Ops:
  0.6 118.8 %shard_map.77 = (f32[1,256,512]{2,1,0:T(8,128)}, f32[8,512]{1,0:T(8,128)}) custom-call(s32[1,2]{1,0:T(1,128)} %blocks.1, f32[1,256]{1,0:T(1,128)} %mass.1, f32[1,256,256]{2,1,0:T(8,128)} %edge_in.1, f32[1,256,256]{2,1,0:T(8,128)} %couple_in.1, f32[1,256,256]{2,1,0:T(8,128)} %topo_in.1, f32[8,512]{1,0:T(8,128)} %gravity.1), custom_call_target="tpu_custom_call" | custom-call | tf_op jit(solution)/shard_map/pallas_call | solution.py:375
  119.5 0.0 copy-start
  119.5 1.9 %copy.10 = f32[1,256,512]{2,1,0:T(8,128)} copy(f32[1,256,512]{2,1,0:T(8,128)} %get-tuple-element.4) | data formatting | bytes 1048576
  121.4 0.0 copy-done
  121.4 0.6 copy.11
Async XLA Ops:
  119.5 1.9 %copy-start = (f32[8,512]{1,0:T(8,128)S(1)}, f32[8,512]{1,0:T(8,128)}, u32[]{:S(2)}) copy-start(f32[8,512]{1,0:T(8,128)} %get-tuple-element.5) | copy-start | bytes 49156

commit v3 on v2

--- a/solution.py
+++ b/solution.py
@@ -27,21 +27,37 @@
     return lax.dot_general(a, b, (((1,), (1,)), ((), ())), precision=HIGHEST, preferred_element_type=F32)
 
 
-def eliminate(cols, rows, lo, nb):
+def eliminate(rows, lo, nb):
+    group = 16
     iota = lax.broadcasted_iota(jnp.int32, (nb, 128), 0)
     lane = lax.broadcasted_iota(jnp.int32, (nb, 128), 1)
     work = [rows, jnp.where(lane == lo + iota, 1.0, 0.0).astype(F32)]
     done = [[], []]
     pivots = []
+    cols = {}
     for k in range(nb):
-        r = k % 8
-        n = nb - 8 * (k // 8)
-        pivot = jnp.broadcast_to(cols[k][r : r + 1, :], (n, 128))
-        pivots.append(pivot[:8])
-        mult = jnp.where(iota[:n] > r, cols[k] * (1.0 / pivot), 0.0)
-        for j in range(k + 1, nb):
-            at = 8 * (j // 8) - 8 * (k // 8)
-            own = j - 8 * (k // 8)
+        r, top = k % 8, 8 * (k // 8)
+        n = nb - top
+        end = k // group * group + group
+        if k % group == 0:
+            for j in range(k, end):
+                at = 8 * (j // 8) - top
+                cols[j] = jnp.broadcast_to(work[0][at:, lo + j : lo + j + 1], (n - at, 128))
+            pivot = jnp.broadcast_to(cols[k][r : r + 1, :], (8, 128))
+        pivots.append(pivot)
+        inverse = 1.0 / pivot
+        mult = cols[k] * (jnp.concatenate([inverse] * (n // 8), 0) if n > 8 else inverse)
+        head = jnp.where(iota[:8] > r, mult[:8], 0.0)
+        mult = jnp.concatenate([head, mult[8:]], 0) if n > 8 else head
+        if k + 1 < end:
+            own = k + 1 - top
+            at = 8 * (own // 8)
+            below = jnp.broadcast_to(cols[k + 1][own - at : own - at + 1, :], (8, 128))
+            beside = jnp.broadcast_to(cols[k][own : own + 1, :], (8, 128))
+            pivot = below - (beside * beside) * inverse
+        for j in range(k + 1, end):
+            own = j - top
+            at = 8 * (own // 8)
             m = jnp.broadcast_to(mult[own : own + 1, :], (n - at, 128))
             cols[j] = cols[j] - cols[k][at:] * m
         for i in range(2):
@@ -59,33 +75,23 @@
     return jnp.concatenate(done[0], 0) * scale, jnp.concatenate(done[1], 0) * scale
 
 
-def small_inverse(mat):
-    nb, n = 32, 128
-    lane = lax.broadcasted_iota(jnp.int32, (nb, n), 1)
-    own = lax.broadcasted_iota(jnp.int32, (nb, n), 0)
-    for p in range(n // nb):
-        k0 = p * nb
-        k1 = k0 + nb
-        rows = mat[k0:k1, :]
-        cols = [
-            jnp.broadcast_to(rows[8 * (j // 8) :, k0 + j : k0 + j + 1], (nb - 8 * (j // 8), n)) for j in range(nb)
-        ]
-        up, unit = eliminate(cols, rows, k0, nb)
-        panel = jnp.where((lane >= k0) & (lane < k1), unit, up)
-
-        def update(a, b):
-            at = lax.broadcasted_iota(jnp.int32, (b - a, n), 1)
-            old = jnp.where((at >= k0) & (at < k1), 0.0, mat[a:b, :])
-            mat[a:b, :] = old - tdot(up[:, a:b], panel)
-
-        if k1 < n:
-            update(k1, k1 + nb)
-        if k1 + nb < n:
-            update(k1 + nb, n)
-        mat[k0:k1, :] = jnp.where(lane <= own + k0, panel, 0.0)
-
-
-def inverse_factor(mat, pair, between=None):
+def small_inverse(mat, between=None):
+    nb = 64
+    lane = lax.broadcasted_iota(jnp.int32, (nb, 128), 1)
+    own = lax.broadcasted_iota(jnp.int32, (nb, 128), 0)
+    up, unit = eliminate(mat[:nb, :], 0, nb)
+    panel = jnp.where(lane < nb, unit, up)
+    old = jnp.where(lane < nb, 0.0, mat[nb:, :])
+    rest = old - tdot(up[:, nb:], panel)
+    mat[:nb, :] = jnp.where(lane <= own, panel, 0.0)
+    if between is not None:
+        between()
+    up, unit = eliminate(rest, nb, nb)
+    panel = jnp.where(lane >= nb, unit, up)
+    mat[nb:, :] = jnp.where(lane <= own + nb, panel, 0.0)
+
+
+def inverse_factor(mat, pair, hooks=None):
     pair[0] = mat[:128, :128]
 
     def middle():
@@ -98,29 +104,29 @@
         pl.when(i == 0)(middle)
         return carry
 
-    if between is None:
+    if hooks is None:
         lax.fori_loop(0, 2, stage, 0)
     else:
-        small_inverse(pair.at[0])
+        small_inverse(pair.at[0], hooks[0])
         middle()
-        between()
-        small_inverse(pair.at[1])
+        hooks[1]()
+        small_inverse(pair.at[1], hooks[2])
     mat[128:, :128] = -dot(pair[1], dot(mat[128:, :128], pair[0]))
     mat[:128, :128] = pair[0]
     mat[128:, 128:] = pair[1]
     mat[:128, 128:] = jnp.zeros((128, 128), F32)
 
 
-def place_columns(compact, ids, first, second):
-    left = jnp.where(ids == first, jnp.concatenate([compact[:, :128]] * 4, 1), 0.0)
-    return left + jnp.where(ids == second, jnp.concatenate([compact[:, 128:]] * 4, 1), 0.0)
+def place_columns(compact, masks):
+    left = jnp.where(masks[0], jnp.concatenate([compact[:, :128]] * 4, 1), 0.0)
+    return left + jnp.where(masks[1], jnp.concatenate([compact[:, 128:]] * 4, 1), 0.0)
 
 
 def whole_kernel(
     blocks, mass, edge_in, couple_in, topo_in, gravity, sens, out,
     edge, edge_behind, couple, topo, weight, diag, right_c, mat, low, up, pair,
     ahead, back, behind, front, right, right_ahead, right_back, right_behind, right_front,
-    half0, half1, cross01, sym, corner, inv, update, remote, local_sem, nsend, nrecv, *rest,
+    tags, tags_behind, tags_front, low_rows, low_rest, half0, half1, cross01, sym, corner, inv, update, remote, local_sem, nsend, nrecv, *rest,
 ):
     strip, harm = lax.axis_index("strip"), lax.axis_index("harm")
     c = lax.rem(strip, 2)
@@ -169,6 +175,14 @@
         for copy in copies:
             copy.wait()
 
+    first, second = blocks[0, 0], blocks[0, 1]
+    tag_row = lax.broadcasted_iota(jnp.int32, (8, HALF), 0)
+    tags[...] = jnp.where(tag_row == 0, first, second).astype(F32)
+    ids = (lax.broadcasted_iota(jnp.int32, (1, HALF), 1) // 128 + harm * 4).astype(F32)
+
+    def masks_of(ref):
+        return [jnp.broadcast_to(ref[i : i + 1, :] == ids, (N, HALF)) for i in range(2)]
+
     weight[...] = tdot(edge[...], edge[...])
     row = lax.broadcasted_iota(jnp.int32, (N, N), 0)
     col = lax.broadcasted_iota(jnp.int32, (N, N), 1)
@@ -176,9 +190,9 @@
     right_c[...] = tdot(couple[...], topo[...])
     pl.semaphore_wait(barrier, len(peers))
     move = push(edge, edge_behind, 0, along(1))
-    ids = lax.broadcasted_iota(jnp.int32, (N, HALF), 1) // 128 + harm * 4
-    first, second = blocks[0, 0], blocks[0, 1]
-    right[...] = place_columns(right_c[...], ids, first, second)
+    tag_moves = [push(tags, tags_behind, 16, along(1)), push(tags, tags_front, 17, along(-1))]
+    masks = masks_of(tags)
+    right[...] = place_columns(right_c[...], masks)
     move.wait()
 
     lower = tdot(edge_behind[...], edge_behind[...])
@@ -197,10 +211,10 @@
     back[1] = tdot(low[...], up[...])
     cross_back = push(back.at[1], front.at[1], 6, along(-1))
     half = dot(mat[...], right_c[...])
-    right_ahead[0] = place_columns(tdot(up[...], half), ids, first, second)
-    right_go = push(right_ahead.at[0], right_behind.at[0], 7, along(1))
-    right_back[0] = place_columns(tdot(low[...], half), ids, first, second)
-    right_come = push(right_back.at[0], right_front.at[0], 8, along(-1))
+    right_ahead[0, :, :N] = tdot(up[...], half)
+    right_go = push(right_ahead.at[0, :, :N], right_behind.at[0, :, :N], 7, along(1))
+    right_back[0, :, :N] = tdot(low[...], half)
+    right_come = push(right_back.at[0, :, :N], right_front.at[0, :, :N], 8, along(-1))
 
     finish(go_ahead + go_back)
     for rows, cols in lower_parts:
@@ -219,7 +233,9 @@
     go_back = push_lower(back.at[2], front.at[2], 11, along(-2))
     right_go.wait()
     right_come.wait()
-    right[...] = right[...] - right_behind[0] - right_front[0]
+    finish(tag_moves)
+    for source, tag in ((right_behind, tags_behind), (right_front, tags_front)):
+        right[...] = right[...] - place_columns(source[0, :, :N], masks_of(tag))
     half = dot(mat[...], right[...])
     right_ahead[1] = tdot(up[...], half)
     right_go = push(right_ahead.at[1], right_behind.at[1], 13, along(2))
@@ -234,12 +250,13 @@
     right_come.wait()
     right[...] = right[...] - right_behind[1] - right_front[1]
     sens[0] = tdot(mat[...], dot(mat[...], right[...]))
-    right[...] = place_columns(topo[...], ids, first, second) - dot(couple[...], sens[0])
+    right[...] = place_columns(topo[...], masks_of(tags)) - dot(couple[...], sens[0])
     right[...] = tdot(topo[...], right[...])
     for b in range(4):
         for shift, part in ((0, half0), (4, half1)):
-            one = jnp.where(ids[:128] * 0 + first == b + shift, right[:128], 0.0)
-            two = jnp.where(ids[:128] * 0 + second == b + shift, right[128:], 0.0)
+            block_id = jnp.float32(b + shift)
+            one = jnp.where(jnp.broadcast_to(tags[0:1, :] == block_id, (128, HALF)), right[:128], 0.0)
+            two = jnp.where(jnp.broadcast_to(tags[1:2, :] == block_id, (128, HALF)), right[128:], 0.0)
             part[128 * b : 128 * b + 128, :] = one + two
     mine = pl.ds(pl.multiple_of(8 * lax.rem(strip, 64), 8), 8)
 
@@ -251,11 +268,12 @@
     def _():
         half1[mine, :] += gravity[...]
 
-    cross01[...] = 0.5 * (half0[N:, :N] + half0[:N, N:].T)
-    chunks = [half0.at[:N, :N], cross01, half0.at[N:, N:], half1.at[:, :N], half1.at[:, N:]]
-    sizes = (N, N, N, HALF, HALF)
-    spaces = [rest[8 * q : 8 * q + 8] for q in range(5)]
-    ssem, rsem = rest[40], rest[41]
+    cross01[:N, :] = 0.5 * (half0[N:, :N] + half0[:N, N:].T)
+    cross01[N:, :] = half0[N:, N:]
+    chunks = [half0.at[:N, :N], cross01, half1.at[:, :N], half1.at[:, N:]]
+    sizes = (N, HALF, HALF, HALF)
+    spaces = [rest[8 * q : 8 * q + 8] for q in range(4)]
+    ssem, rsem = rest[32], rest[33]
     mine_lanes = pl.ds(pl.multiple_of(c * 128, 128), 128)
     other_lanes = pl.ds(pl.multiple_of((1 - c) * 128, 128), 128)
 
@@ -314,39 +332,68 @@
         return spread(q, slice(None), mine_lanes, 22, [core])
 
     steps = (sum_core, sum_x, sum_z, sum_y, spread_z, spread_x, spread_core)
-    live = [[], [], [], [], []]
-
-    def tick(t):
-        for q in range(5):
-            s = t - q
-            if 0 <= s <= len(steps):
-                finish(live[q])
-                live[q] = steps[s](q) if s < len(steps) else []
-
-    for t in range(8):
-        tick(t)
+    live = [[], [], [], []]
+
+    def advance(q, s):
+        finish(live[q])
+        live[q] = steps[s](q) if s < len(steps) else []
+
+    for t in range(6):
+        for q in range(4):
+            if t >= q:
+                advance(q, t - q)
+    advance(0, 6)
+    advance(0, 7)
 
     full = [space[7] for space in spaces]
     sym[:N, :N] = 0.5 * (full[0][...] + full[0][...].T)
-    sym[:N, N:] = jnp.zeros((N, N), F32)
     corner[0] = sym[:N, :N]
-    inverse_factor(corner.at[0], pair, lambda: tick(8))
-    tick(9)
-    sym[N:, :N] = full[1][...]
-    sym[N:, N:] = 0.5 * (full[2][...] + full[2][...].T)
-    inv[:N, N:] = dott(sym[N:, :N], corner[0])
-    corner[1] = sym[N:, N:] - dott(inv[:N, N:], inv[:N, N:])
-    inverse_factor(corner.at[1], pair, lambda: tick(10))
-    tick(11)
-    inv[N:, :N] = -dot(corner[1], dot(inv[:N, N:], corner[0]))
-    inv[:N, :N] = corner[0]
-    inv[N:, N:] = corner[1]
-    inv[:N, N:] = jnp.zeros((N, N), F32)
-    bottom_rows = jnp.concatenate([full[3][mine, :], full[4][mine, :]], 1)
-    source = jnp.where(strip < 64, sym[mine, :], bottom_rows)
-    solved = dott(source, inv[...])
-    back_solved = dot(solved, inv[...])
-    update[...] = dott(back_solved[:, :N], full[3][...]) + dott(back_solved[:, N:], full[4][...])
+
+    def hook_first():
+        advance(1, 5)
+        advance(2, 4)
+        advance(3, 3)
+
+    def hook_second():
+        advance(1, 6)
+        advance(2, 5)
+        advance(3, 4)
+
+    def nothing():
+        pass
+
+    inverse_factor(corner.at[0], pair, (hook_first, nothing, hook_second))
+    advance(1, 7)
+    inv[N:, :N] = dott(full[1][:N, :], corner[0])
+    schur = 0.5 * (full[1][N:, :] + full[1][N:, :].T) - dott(inv[N:, :N], inv[N:, :N])
+    inv[N:, N:] = schur
+    corner[1] = schur
+
+    def hook_third():
+        advance(2, 6)
+        advance(3, 5)
+
+    def hook_fourth():
+        advance(2, 7)
+        low_rows[...] = dott(full[2][...], corner[0])
+
+    def hook_last():
+        advance(3, 6)
+
+    inverse_factor(corner.at[1], pair, (hook_third, hook_fourth, hook_last))
+    advance(3, 7)
+    low_rest[...] = full[3][...] - dott(low_rows[...], inv[N:, :N])
+    quarter = pl.ds(pl.multiple_of(8 * lax.rem(strip, 32), 8), 8)
+    top_rows = dott(sym[quarter, :N], corner[0])
+    upper_part, lower_part = strip < 32, strip < 64
+    solved1 = jnp.where(
+        upper_part, top_rows, jnp.where(lower_part, inv[pl.ds(pl.multiple_of(N + 8 * lax.rem(strip, 32), 8), 8), :N], low_rows[mine, :])
+    )
+    rest2 = jnp.where(lower_part, inv[pl.ds(pl.multiple_of(N + 8 * lax.rem(strip, 32), 8), 8), N:], low_rest[mine, :])
+    solved2 = dott(rest2, corner[1])
+    update[...] = dott(solved1, low_rows[...]) + dott(dot(solved2, corner[1]), low_rest[...])
+    solved = jnp.concatenate([solved1, solved2], 1)
+    bottom_rows = jnp.concatenate([full[2][mine, :], full[3][mine, :]], 1)
     cross_over = push(update, remote, 15, mirror)
     at_row = lax.broadcasted_iota(jnp.int32, (8, HALF), 0) + 8 * lax.rem(strip, 64)
     at_col = lax.broadcasted_iota(jnp.int32, (8, HALF), 1)
@@ -366,12 +413,13 @@
     scratch = [v(N, N)] * 2 + [v(N, N)] * 8 + [v(2, 128, 128)]
     scratch += [v(3, N, N)] * 4 + [v(N, HALF)] + [v(2, N, HALF)] * 4
     dma = pltpu.SemaphoreType.DMA
-    scratch += [v(HALF, HALF), v(HALF, HALF), v(N, N), v(HALF, HALF), v(2, N, N), v(HALF, HALF), v(8, HALF), v(8, HALF)]
-    scratch += [dma((3,)), dma((16,)), dma((16,))]
-    for n in (N, N, N, HALF, HALF):
+    scratch += [v(8, HALF)] * 3 + [v(HALF, N)] * 2
+    scratch += [v(HALF, HALF), v(HALF, HALF), v(HALF, N), v(HALF, HALF), v(2, N, N), v(HALF, HALF), v(8, HALF), v(8, HALF)]
+    scratch += [dma((3,)), dma((18,)), dma((18,))]
+    for n in (N, HALF, HALF, HALF):
         m, k = n // NX, n // NX // NZ
         scratch += [v(n, 128), v(n, 128), v(3, m, 128), v(m, 128), v(7, k, 128), v(k, 128), v(k, 128), v(n, N)]
-    scratch += [dma((5, 23)), dma((5, 23))]
+    scratch += [dma((4, 23)), dma((4, 23))]
     return pl.pallas_call(
         whole_kernel,
         out_shape=(jax.ShapeDtypeStruct((1, N, HALF), F32), jax.ShapeDtypeStruct((8, HALF), F32)),

time: 124 us -> 115 us (0.927)
  Pallas kernels: 119 us -> 109 us
    pallas_call x1, Pallas kernels: 119 us -> 109 us  [shards(): pl.pallas_call(whole_kernel, out_shape=(jax.ShapeDtypeStruct((1, N, HALF)...]
where the time goes in v3:
time: 115 us; the launch traced here: 113 us
  Pallas kernels  109 us (95%)
  local copies, waits for them, and re-layouts  2.48 us (2%)
    pallas_call x1, Pallas kernels, shards(): pl.pallas_call(whole_kernel, out_shape=(jax.ShapeDtypeStruct((1, N, HALF)...  109 us
    unnamed x4, local copies, waits for them, and re-layouts  2.48 us

profile of v3, /device:TPU:24, one launch (start us, length us, event | category | flops | bytes accessed | tf_op | source)
XLA Modules:
  0.0 112.5 jit_solution(15319204663794440865)
XLA Ops:
  0.6 109.4 %shard_map.77 = (f32[1,256,512]{2,1,0:T(8,128)}, f32[8,512]{1,0:T(8,128)}) custom-call(s32[1,2]{1,0:T(1,128)} %blocks.1, f32[1,256]{1,0:T(1,128)} %mass.1, f32[1,256,256]{2,1,0:T(8,128)} %edge_in.1, f32[1,256,256]{2,1,0:T(8,128)} %couple_in.1, f32[1,256,256]{2,1,0:T(8,128)} %topo_in.1, f32[8,512]{1,0:T(8,128)} %gravity.1), custom_call_target="tpu_custom_call" | custom-call | tf_op jit(solution)/shard_map/pallas_call | solution.py:423
  110.0 0.0 copy-start
  110.0 1.9 %copy.10 = f32[1,256,512]{2,1,0:T(8,128)} copy(f32[1,256,512]{2,1,0:T(8,128)} %get-tuple-element.4) | data formatting | bytes 1048576
  111.9 0.0 copy-done
  111.9 0.6 copy.11
Async XLA Ops:
  110.0 1.9 %copy-start = (f32[8,512]{1,0:T(8,128)S(1)}, f32[8,512]{1,0:T(8,128)}, u32[]{:S(2)}) copy-start(f32[8,512]{1,0:T(8,128)} %get-tuple-element.5) | copy-start | bytes 49156

commit v4 on v3

--- a/solution.py
+++ b/solution.py
@@ -27,7 +27,7 @@
     return lax.dot_general(a, b, (((1,), (1,)), ((), ())), precision=HIGHEST, preferred_element_type=F32)
 
 
-def eliminate(rows, lo, nb):
+def eliminate(rows, lo, nb, hooks):
     group = 16
     iota = lax.broadcasted_iota(jnp.int32, (nb, 128), 0)
     lane = lax.broadcasted_iota(jnp.int32, (nb, 128), 1)
@@ -40,6 +40,7 @@
         n = nb - top
         end = k // group * group + group
         if k % group == 0:
+            hooks[k // group]()
             for j in range(k, end):
                 at = 8 * (j // 8) - top
                 cols[j] = jnp.broadcast_to(work[0][at:, lo + j : lo + j + 1], (n - at, 128))
@@ -75,18 +76,20 @@
     return jnp.concatenate(done[0], 0) * scale, jnp.concatenate(done[1], 0) * scale
 
 
-def small_inverse(mat, between=None):
+def idle():
+    pass
+
+
+def small_inverse(mat, hooks=(idle,) * 8):
     nb = 64
     lane = lax.broadcasted_iota(jnp.int32, (nb, 128), 1)
     own = lax.broadcasted_iota(jnp.int32, (nb, 128), 0)
-    up, unit = eliminate(mat[:nb, :], 0, nb)
+    up, unit = eliminate(mat[:nb, :], 0, nb, hooks[:4])
     panel = jnp.where(lane < nb, unit, up)
     old = jnp.where(lane < nb, 0.0, mat[nb:, :])
     rest = old - tdot(up[:, nb:], panel)
     mat[:nb, :] = jnp.where(lane <= own, panel, 0.0)
-    if between is not None:
-        between()
-    up, unit = eliminate(rest, nb, nb)
+    up, unit = eliminate(rest, nb, nb, hooks[4:])
     panel = jnp.where(lane >= nb, unit, up)
     mat[nb:, :] = jnp.where(lane <= own + nb, panel, 0.0)
 
@@ -107,10 +110,9 @@
     if hooks is None:
         lax.fori_loop(0, 2, stage, 0)
     else:
-        small_inverse(pair.at[0], hooks[0])
+        small_inverse(pair.at[0], hooks[:8])
         middle()
-        hooks[1]()
-        small_inverse(pair.at[1], hooks[2])
+        small_inverse(pair.at[1], hooks[8:])
     mat[128:, :128] = -dot(pair[1], dot(mat[128:, :128], pair[0]))
     mat[:128, :128] = pair[0]
     mat[128:, 128:] = pair[1]
@@ -123,10 +125,10 @@
 
 
 def whole_kernel(
-    blocks, mass, edge_in, couple_in, topo_in, gravity, sens, out,
-    edge, edge_behind, couple, topo, weight, diag, right_c, mat, low, up, pair,
+    blocks, mass, edge_in, couple_in, topo_in, gravity, sens_out, out,
+    edge, behind_weight, couple, topo, weight, diag, right_c, mat, low, up, pair,
     ahead, back, behind, front, right, right_ahead, right_back, right_behind, right_front,
-    tags, tags_behind, tags_front, low_rows, low_rest, half0, half1, cross01, sym, corner, inv, update, remote, local_sem, nsend, nrecv, *rest,
+    sens, tags, tags_behind, tags_front, low_rows, low_rest, half0, half1, cross01, sym, corner, inv, update, remote, local_sem, nsend, nrecv, sens_sem, *rest,
 ):
     strip, harm = lax.axis_index("strip"), lax.axis_index("harm")
     c = lax.rem(strip, 2)
@@ -144,10 +146,10 @@
     core = at(x, yh, z, 1 - c)
     xs = [at(lax.rem(x + d, NX), yh, z, c) for d in range(1, NX)]
     zs = [at(x, yh, lax.rem(z + d, NZ), c) for d in range(1, NZ)]
-    ys = at(x, 1 - yh, z, c)
+    os = [at(x, 1 - yh, lax.rem(z + d, NZ), c) for d in range(NZ)]
     mirror = (strip, 1 - harm)
     barrier = pltpu.get_barrier_semaphore()
-    peers = [along(1), along(-1), along(2), along(-2), core, ys, mirror] + xs + zs
+    peers = [along(1), along(-1), along(2), along(-2), core, mirror] + xs + zs + os
     for peer in peers:
         pl.semaphore_signal(barrier, inc=1, device_id=peer, device_id_type=MESH)
     loads = [
@@ -189,18 +191,17 @@
     diag[...] = weight[...] + tdot(couple[...], couple[...]) + jnp.where(row == col, mass[...], 0.0)
     right_c[...] = tdot(couple[...], topo[...])
     pl.semaphore_wait(barrier, len(peers))
-    move = push(edge, edge_behind, 0, along(1))
+    move = push_lower(weight, behind_weight, 18, along(1))
     tag_moves = [push(tags, tags_behind, 16, along(1)), push(tags, tags_front, 17, along(-1))]
     masks = masks_of(tags)
     right[...] = place_columns(right_c[...], masks)
-    move.wait()
-
-    lower = tdot(edge_behind[...], edge_behind[...])
-    diag[...] = diag[...] + lower
+    finish(move)
+
+    behind_weight[:128, 128:] = behind_weight[128:, :128].T
+    diag[...] = diag[...] + behind_weight[...]
     mat[...] = diag[...]
-    edge_behind[...] = lower
     inverse_factor(mat, pair)
-    low[...] = -dot(mat[...], edge_behind[...])
+    low[...] = -dot(mat[...], behind_weight[...])
     up[...] = -dot(mat[...], weight[...])
     ahead[0] = tdot(up[...], up[...])
     go_ahead = push_lower(ahead.at[0], behind.at[0], 1, along(1))
@@ -249,8 +250,10 @@
     right_go.wait()
     right_come.wait()
     right[...] = right[...] - right_behind[1] - right_front[1]
-    sens[0] = tdot(mat[...], dot(mat[...], right[...]))
-    right[...] = place_columns(topo[...], masks_of(tags)) - dot(couple[...], sens[0])
+    sens[...] = tdot(mat[...], dot(mat[...], right[...]))
+    right[...] = place_columns(topo[...], masks_of(tags)) - dot(couple[...], sens[...])
+    sens_write = pltpu.make_async_copy(sens, sens_out.at[0], sens_sem)
+    sens_write.start()
     right[...] = tdot(topo[...], right[...])
     for b in range(4):
         for shift, part in ((0, half0), (4, half1)):
@@ -307,82 +310,92 @@
             send(q, wx.at[block(lax.rem(z + d, NZ), size)], bz.at[d - 1], 3 + d, zs[d - 1]) for d in range(1, NZ)
         ]
 
-    def sum_y(q):
-        wx, bz, wz, by = spaces[q][3:7]
-        total = wx[block(z, sizes[q] // NX // NZ), :]
+    def spread_plane(q):
+        wx, bz, own, other = spaces[q][3:7]
+        piece = block(z, sizes[q] // NX // NZ)
+        total = wx[piece, :]
         for d in range(1, NZ):
             total = total + bz[d - 1]
-        wz[...] = total
-        return [send(q, wz, by, 11, ys)]
-
-    def spread(q, piece, lanes, slot, targets):
-        view = spaces[q][7].at[piece, lanes]
+        own[piece, :] = total
+        here = [send(q, own.at[piece], own.at[piece], 11 + i, peer) for i, peer in enumerate(zs)]
+        return here + [send(q, own.at[piece], other.at[piece], 18 + i, peer) for i, peer in enumerate(os)]
+
+    def spread(q, piece, slot, targets):
+        view = spaces[q][7].at[piece, mine_lanes]
         return [send(q, view, view, slot + i, peer) for i, peer in enumerate(targets)]
 
-    def spread_z(q):
-        wz, by, full = spaces[q][5:8]
-        piece = block(x * NZ + z, sizes[q] // NX // NZ)
-        full[piece, mine_lanes] = wz[...] + by[...]
-        return spread(q, piece, mine_lanes, 12, zs)
-
     def spread_x(q):
-        return spread(q, block(x, sizes[q] // NX), mine_lanes, 19, xs)
+        own, other, full = spaces[q][5:8]
+        piece = block(x, sizes[q] // NX)
+        full[piece, mine_lanes] = own[...] + other[...]
+        return spread(q, piece, 26, xs)
 
     def spread_core(q):
-        return spread(q, slice(None), mine_lanes, 22, [core])
-
-    steps = (sum_core, sum_x, sum_z, sum_y, spread_z, spread_x, spread_core)
+        return spread(q, slice(None), 29, [core])
+
+    steps = (sum_core, sum_x, sum_z, spread_plane, spread_x, spread_core)
     live = [[], [], [], []]
 
     def advance(q, s):
         finish(live[q])
         live[q] = steps[s](q) if s < len(steps) else []
 
-    for t in range(6):
-        for q in range(4):
-            if t >= q:
-                advance(q, t - q)
+    advance(0, 0)
+    advance(1, 0)
+    advance(2, 0)
+    advance(3, 0)
+    advance(0, 1)
+    advance(1, 1)
+    advance(0, 2)
+    advance(2, 1)
+    advance(3, 1)
+    advance(0, 3)
+    advance(1, 2)
+    advance(2, 2)
+    advance(3, 2)
+    advance(0, 4)
+    advance(1, 3)
+    advance(2, 3)
+    advance(3, 3)
+    advance(0, 5)
     advance(0, 6)
-    advance(0, 7)
 
     full = [space[7] for space in spaces]
     sym[:N, :N] = 0.5 * (full[0][...] + full[0][...].T)
     corner[0] = sym[:N, :N]
 
-    def hook_first():
-        advance(1, 5)
-        advance(2, 4)
-        advance(3, 3)
-
-    def hook_second():
-        advance(1, 6)
-        advance(2, 5)
-        advance(3, 4)
-
-    def nothing():
-        pass
-
-    inverse_factor(corner.at[0], pair, (hook_first, nothing, hook_second))
-    advance(1, 7)
+    early = [idle] * 16
+
+    def early_7():
+        advance(1, 4)
+
+    early[7] = early_7
+    inverse_factor(corner.at[0], pair, early)
+    advance(1, 5)
+    advance(2, 4)
+    advance(3, 4)
+    advance(1, 6)
     inv[N:, :N] = dott(full[1][:N, :], corner[0])
     schur = 0.5 * (full[1][N:, :] + full[1][N:, :].T) - dott(inv[N:, :N], inv[N:, :N])
     inv[N:, N:] = schur
     corner[1] = schur
 
-    def hook_third():
+    late = [idle] * 16
+
+    def late_10():
+        advance(2, 5)
+        advance(3, 5)
+
+    late[10] = late_10
+
+    def late_15():
         advance(2, 6)
-        advance(3, 5)
-
-    def hook_fourth():
-        advance(2, 7)
+        advance(3, 6)
         low_rows[...] = dott(full[2][...], corner[0])
-
-    def hook_last():
-        advance(3, 6)
-
-    inverse_factor(corner.at[1], pair, (hook_third, hook_fourth, hook_last))
-    advance(3, 7)
-    low_rest[...] = full[3][...] - dott(low_rows[...], inv[N:, :N])
+        low_rest[...] = full[3][...] - dott(low_rows[...], inv[N:, :N])
+
+    late[15] = late_15
+    inverse_factor(corner.at[1], pair, late)
     quarter = pl.ds(pl.multiple_of(8 * lax.rem(strip, 32), 8), 8)
     top_rows = dott(sym[quarter, :N], corner[0])
     upper_part, lower_part = strip < 32, strip < 64
@@ -399,6 +412,7 @@
     at_col = lax.broadcasted_iota(jnp.int32, (8, HALF), 1)
     solved = jnp.where((strip >= 64) | (at_col <= at_row), solved, 0.0)
     cross_over.wait()
+    sens_write.wait()
     trailing = jnp.where(strip < 64, 0.0, bottom_rows - remote[...])
     out[...] = jnp.where(harm == 0, solved, trailing)
 
@@ -413,18 +427,18 @@
     scratch = [v(N, N)] * 2 + [v(N, N)] * 8 + [v(2, 128, 128)]
     scratch += [v(3, N, N)] * 4 + [v(N, HALF)] + [v(2, N, HALF)] * 4
     dma = pltpu.SemaphoreType.DMA
-    scratch += [v(8, HALF)] * 3 + [v(HALF, N)] * 2
+    scratch += [v(N, HALF)] + [v(8, HALF)] * 3 + [v(HALF, N)] * 2
     scratch += [v(HALF, HALF), v(HALF, HALF), v(HALF, N), v(HALF, HALF), v(2, N, N), v(HALF, HALF), v(8, HALF), v(8, HALF)]
-    scratch += [dma((3,)), dma((18,)), dma((18,))]
+    scratch += [dma((3,)), dma((20,)), dma((20,)), dma]
     for n in (N, HALF, HALF, HALF):
         m, k = n // NX, n // NX // NZ
-        scratch += [v(n, 128), v(n, 128), v(3, m, 128), v(m, 128), v(7, k, 128), v(k, 128), v(k, 128), v(n, N)]
-    scratch += [dma((4, 23)), dma((4, 23))]
+        scratch += [v(n, 128), v(n, 128), v(3, m, 128), v(m, 128), v(7, k, 128), v(m, 128), v(m, 128), v(n, N)]
+    scratch += [dma((4, 30)), dma((4, 30))]
     return pl.pallas_call(
         whole_kernel,
         out_shape=(jax.ShapeDtypeStruct((1, N, HALF), F32), jax.ShapeDtypeStruct((8, HALF), F32)),
         in_specs=[pl.BlockSpec(memory_space=pltpu.SMEM), vmem, hbm, hbm, hbm, vmem],
-        out_specs=(vmem, vmem),
+        out_specs=(hbm, vmem),
         scratch_shapes=scratch,
         compiler_params=pltpu.CompilerParams(vmem_limit_bytes=60 << 20, collective_id=0, has_side_effects=True),
     )(col_blocks, mass, edge_map, couple_map, topo_rows, gravity)

time: 115 us -> 113 us (0.983); the launches traced: 113 us -> 112 us
  no operation moved by 1% of the time
where the time goes in v4:
time: 113 us; the launch traced here: 112 us
  Pallas kernels  109 us (96%)
  local copies, waits for them, and re-layouts  2.48 us (2%)
    pallas_call x1, Pallas kernels, shards(): pl.pallas_call(whole_kernel, out_shape=(jax.ShapeDtypeStruct((1, N, HALF)...  109 us
    unnamed x4, local copies, waits for them, and re-layouts  2.48 us

profile of v4, /device:TPU:24, one launch (start us, length us, event | category | flops | bytes accessed | tf_op | source)
XLA Modules:
  0.0 112.0 jit_solution(7956952569931002770)
XLA Ops:
  0.6 108.9 %shard_map.77 = (f32[1,256,512]{2,1,0:T(8,128)}, f32[8,512]{1,0:T(8,128)}) custom-call(s32[1,2]{1,0:T(1,128)} %blocks.1, f32[1,256]{1,0:T(1,128)} %mass.1, f32[1,256,256]{2,1,0:T(8,128)} %edge_in.1, f32[1,256,256]{2,1,0:T(8,128)} %couple_in.1, f32[1,256,256]{2,1,0:T(8,128)} %topo_in.1, f32[8,512]{1,0:T(8,128)} %gravity.1), custom_call_target="tpu_custom_call" | custom-call | tf_op jit(solution)/shard_map/pallas_call | solution.py:437
  109.5 0.0 copy-start
  109.5 1.9 %copy.10 = f32[1,256,512]{2,1,0:T(8,128)} copy(f32[1,256,512]{2,1,0:T(8,128)} %get-tuple-element.4) | data formatting | bytes 1048576
  111.4 0.0 copy-done
  111.4 0.6 copy.11
Async XLA Ops:
  109.5 1.9 %copy-start = (f32[8,512]{1,0:T(8,128)S(1)}, f32[8,512]{1,0:T(8,128)}, u32[]{:S(2)}) copy-start(f32[8,512]{1,0:T(8,128)} %get-tuple-element.5) | copy-start | bytes 49156
